TPU v7x, 128 devices: a whole 4x4x4 slice. The times are simulated.
128 devices in a mesh: row: 16 (over y, z_lo, core), col: 8 (over z_hi, x).
Axes of the slice: x: 4, y: 4, z: 4 (z_hi: 2, z_lo: 2; z = z_hi * 2 + z_lo), core: 2. Of those that a mesh axis runs over, the one named last changes fastest.
Arguments:
- samples: bfloat16 [32768, 8192], P(('row', 'col'))
- labels: int32 [32768], P(('row', 'col')), may hold values from 0 to 1
- basis_start: bfloat16 [8192, 256], replicated, may hold values from -0.0625 to 0.0625
- width_index: int32 [], replicated, may hold values from 0 to 2
Outputs:
- projected: bfloat16 [32768, 256], P(('row', 'col'))
- proof: float32 [32768], P(('row', 'col'))
- basis: bfloat16 [8192, 256], replicated
All inputs are finite; a program needn't handle non-finite values.
Results may differ from a plain program's by a relative error of at most 0.011.
Values may be sent and summed in bfloat16 or wider, within the bound.
A program may use at most 128 MiB of HBM per device.

v0:
```python
import math
import jax
import jax.numpy as jnp
from jax import lax
from jax.sharding import PartitionSpec as P


def kernel_sums(panel_rows, panel_cols, col_is_ref, width_sq):
    row_norms = jnp.sum(jnp.square(panel_rows.astype(jnp.float32)), 1)
    col_norms = jnp.sum(jnp.square(panel_cols.astype(jnp.float32)), 1)
    block_size = math.gcd(panel_rows.shape[0], 512)

    def block_sums(pieces):
        block_rows, block_norms = pieces
        inner_products = lax.dot_general(
            block_rows, panel_cols, (((1,), (1,)), ((), ())), preferred_element_type=jnp.float32
        )
        dist_sq = block_norms[:, None] + col_norms[None, :] - 2.0 * inner_products
        kernel = jnp.exp(-dist_sq / (2.0 * width_sq))
        return (jnp.sum(kernel * col_is_ref[None, :], 1), jnp.sum(kernel, 1))

    ref_sums, row_sums = lax.map(
        block_sums,
        (
            panel_rows.reshape(-1, block_size, panel_rows.shape[1]),
            row_norms.reshape(-1, block_size),
        ),
    )
    return (ref_sums.reshape(-1), row_sums.reshape(-1))


def local(samples, labels, basis_start, width_index):
    n_total = jnp.float32(samples.shape[0] * lax.axis_size(("row", "col")))
    is_ref = (labels == 0).astype(jnp.float32)
    column_total, n_ref = lax.psum(
        (jnp.sum(samples, 0, dtype=jnp.float32), jnp.sum(is_ref)), ("row", "col")
    )
    n_cur = n_total - n_ref
    sample_mean = column_total / n_total
    centred = (samples - sample_mean).astype(jnp.bfloat16)
    first = jnp.dot(centred, basis_start, preferred_element_type=jnp.float32).astype(jnp.bfloat16)
    gram_part = (
        lax.dot_general(
            centred, first, (((0,), (0,)), ((), ())), preferred_element_type=jnp.float32
        )
        / n_total
    )
    gram = lax.psum(gram_part, ("row", "col"))
    square = jnp.dot(gram.T, gram, precision=lax.Precision.HIGHEST)
    factor = jnp.linalg.cholesky(square)
    basis = jax.scipy.linalg.solve_triangular(factor, gram.T, lower=True).T.astype(jnp.bfloat16)
    projected = jnp.dot(centred, basis, preferred_element_type=jnp.float32).astype(jnp.bfloat16)
    width_sq = 128.0 * jnp.exp2(width_index.astype(jnp.float32))
    panel_rows = lax.all_gather(projected, "col", axis=0, tiled=True)
    panel_cols, col_is_ref = (
        lax.all_gather(projected, "row", axis=0, tiled=True),
        lax.all_gather(is_ref.astype(jnp.bfloat16), "row", axis=0, tiled=True).astype(is_ref.dtype),
    )
    part_ref, part_rows = kernel_sums(panel_rows, panel_cols, col_is_ref, width_sq)
    ref_sums, row_sums = (
        lax.psum_scatter(part_ref, "col", scatter_dimension=0, tiled=True),
        lax.psum_scatter(part_rows, "col", scatter_dimension=0, tiled=True),
    )
    proof = (ref_sums / n_ref - (row_sums - ref_sums) / n_cur) / (row_sums / n_total)
    return (projected, proof, basis)


def solution(mesh):
    placed = (P(("row", "col"), None), P(("row", "col")), P(), P())
    return jax.shard_map(
        local,
        mesh=mesh,
        in_specs=placed,
        out_specs=(P(("row", "col"), None), P(("row", "col")), P()),
        check_vma=False,
    )
```

profile of v0, /device:TPU:0, one launch (start us, length us, event | category | flops | bytes accessed | tf_op | source)
XLA Modules:
  0.0 501.4 jit_solution(13970861167934475783)
XLA Ops:
  7.2 0.0 copy-start.3
  7.2 0.0 all-reduce.7.cloned.1.call-start
  7.2 2.9 convert_reduce_fusion
  10.1 0.0 copy-done.3
  10.1 0.6 fusion.26
  10.7 68.6 %all-reduce.3 = (f32[8192]{0:T(1024)S(1)}, f32[]{:T(128)}) all-reduce(f32[8192]{0:T(1024)S(1)} %convert_reduce_fusion, f32[]{:T(128)} %fusion.26), channel_id=1, replica_groups=mesh['row'=16,'col'=8] {'row','col'}, use_global_device_ids=true, to_apply=%region_1.0 | all-reduce | flops 8193 | bytes 65544 | tf_op jit(solution)/shard_map/psum | solution.py:35
  79.3 12.5 %convolution_multiply_fusion = f32[8192,256]{1,0:T(8,128)} fusion(bf16[256,8192]{1,0:T(8,128)(2,1)} %param.6, f32[8192]{0:T(1024)S(1)} %broadcast_multiply_fusion, bf16[8192,256]{1,0:T(8,128)(2,1)} %param.8), kind=kOutput, calls=%fused_computation.8 | convolution fusion | flops 2162229248 | bytes 16809984 | tf_op jit(solution)/shard_map/dot_general | solution.py:43
  91.8 0.0 all-reduce.7.cloned.1.call-update
  91.8 0.3 all-gather.4.cloned.1.call-start
  92.2 157.7 %all-reduce.7.cloned.1.call-done = f32[8192,256]{1,0:T(8,128)} async-done(((f32[8192,256]{1,0:T(8,128)}), f32[8192,256]{1,0:T(8,128)}) %all-reduce.7.cloned.1.call-update) | async-done | bytes 8388624 | tf_op jit(solution)/shard_map/psum | solution.py:48
  249.9 19.5 %fusion.32 = f32[256,256]{1,0:T(8,128)S(1)} fusion(f32[8192,256]{1,0:T(8,128)} %all-reduce.7.cloned.1.call-done), kind=kOutput, calls=%fused_computation.55 | convolution fusion | flops 6442450944 | bytes 8650752 | tf_op jit(solution)/shard_map/dot_general | solution.py:49
  269.5 0.1 copy.9
  269.7 11.7 %cholesky.50 = f32[128,128]{1,0:T(8,128)S(1)} custom-call(f32[128,128]{1,0:T(8,128)S(1)} %cholesky.118), custom_call_target="Cholesky" | custom-call | tf_op jit(solution)/shard_map/jit(cholesky)/cholesky | solution.py:50
  281.4 9.8 %custom-call.15 = f32[1,128,128]{1,2,0:T(8,128)S(1)} custom-call(f32[1,128,128]{2,1,0:T(8,128)S(1)} %get-tuple-element.162), custom_call_target="InvertDiagBlocksLowerTriangular" | custom-call | tf_op jit(solution)/shard_map/jit(cholesky)/cholesky | solution.py:50
  291.3 0.2 constant_dynamic-update-slice_fusion.1
  291.5 0.3 convolution_subtract_fusion.1
  291.8 11.7 %cholesky.105 = f32[128,128]{1,0:T(8,128)S(1)} custom-call(f32[128,128]{1,0:T(8,128)S(1)} %convolution_subtract_fusion.1), custom_call_target="Cholesky" | custom-call | tf_op jit(solution)/shard_map/jit(cholesky)/cholesky | solution.py:50
  303.5 0.6 compare_reduce_fusion
  305.5 0.1 triangular_solve.59
  305.6 4.0 while.16
  305.6 0.6 fusion.46
  306.1 1.4 bitcast_dynamic-update-slice_fusion.2
  307.6 0.6 fusion.46
  308.2 1.4 bitcast_dynamic-update-slice_fusion.2
  309.5 19.8 %custom-call.16 = f32[2,128,128]{1,2,0:T(8,128)S(1)} custom-call(f32[2,128,128]{2,1,0:T(8,128)S(1)} %get-tuple-element.118), custom_call_target="InvertDiagBlocksLowerTriangular" | custom-call | tf_op jit(solution)/shard_map/jit(_solve_triangular)/triangular_solve | solution.py:51
  329.4 0.0 copy-start
  329.4 5.7 %fusion.31 = (bf16[128,8192]{1,0:T(8,128)(2,1)S(1)}, f32[128,8192]{1,0:T(8,128)S(1)}) fusion(f32[256,8192]{0,1:T(8,128)} %bitcast.65, f32[2,128,128]{1,2,0:T(8,128)S(1)} %custom-call.16), kind=kOutput, calls=%fused_computation.54 | convolution fusion | flops 1611661312 | bytes 10551296 | tf_op jit(solution)/shard_map/jit(_solve_triangular)/triangular_solve | solution.py:51
  335.1 0.0 copy-done
  335.1 6.7 %convolution_subtract_fusion = f32[128,8192]{0,1:T(8,128)S(1)} fusion(f32[128,8192]{1,0:T(8,128)S(1)} %get-tuple-element.166, f32[256,8192]{0,1:T(8,128)S(1)} %bitcast.66, f32[256,256]{1,0:T(8,128)S(1)} %get-tuple-element.312), kind=kOutput, calls=%fused_computation.11 | convolution fusion | flops 1611661312 | bytes 12648448 | tf_op jit(solution)/shard_map/jit(_solve_triangular)/triangular_solve | solution.py:51
  341.8 0.0 copy-start.1
  341.8 4.1 convolution_convert_fusion
  345.9 0.0 copy-start.2
  345.9 1.3 copy-done.2
  347.3 0.0 copy-done.1
  347.3 0.0 copy-start.4
  347.3 2.1 fusion.15
  349.4 0.0 all-gather.4.cloned.1.call-update
  349.4 0.0 all-gather.6.cloned.1.call-start
  349.5 0.7 all-gather.6.cloned.1.call-update
  350.2 17.6 %all-gather = bf16[16,1,256]{2,1,0:T(2,128)(2,1)S(1)} all-gather(bf16[1,1,256]{2,1,0:T(2,128)(2,1)S(1)} %reshape.65), channel_id=1, replica_groups=mesh['row'=16,'col'=8] {'row'}, dimensions={0}, use_global_device_ids=true | all-gather | bytes 8704 | tf_op jit(solution)/shard_map/all_gather | solution.py:57
  369.0 0.0 copy-done.4
  369.1 0.7 dynamic-slice.3
  370.4 3.9 fusion.11
  374.3 6.4 %copy.10 = bf16[8192,256]{1,0:T(8,128)(2,1)} copy(bf16[8192,256]{0,1:T(8,128)(2,1)} %fusion.11) | data formatting | bytes 8388608
  380.7 14.3 %all-gather.4.cloned.1.call-done = bf16[2048,256]{1,0:T(8,128)(2,1)} async-done(((bf16[256,256]{1,0:T(8,128)(2,1)}), bf16[2048,256]{1,0:T(8,128)(2,1)}) %all-gather.4.cloned.1.call-update) | async-done | bytes 1048592 | tf_op jit(solution)/shard_map/all_gather | solution.py:54
  394.9 1.6 multiply_reduce_fusion.2
  396.5 33.2 %all-gather.6.cloned.1.call-done = bf16[4096,256]{1,0:T(8,128)(2,1)} async-done(((bf16[256,256]{1,0:T(8,128)(2,1)}), bf16[4096,256]{1,0:T(8,128)(2,1)}) %all-gather.6.cloned.1.call-update) | async-done | bytes 2097168 | tf_op jit(solution)/shard_map/all_gather | solution.py:56
  429.7 2.2 multiply_reduce_fusion.1
  431.9 19.9 %while.15 = (s32[]{:T(128)}, f32[4,512]{1,0:T(4,128)S(1)}, f32[4,512]{1,0:T(4,128)S(1)}, f32[4,512]{1,0:T(4,128)S(1)}, f32[4096]{0:T(1024)S(1)}, /*index=5*/bf16...) while((s32[]{:T(128)}, f32[4,512]{1,0:T(4,128)S(1)}, ...), condition=%wide.region_12.13_spmd, body=%wide.region_9.12_spmd.sunk | while | flops 1090518016 | bytes 2411641 | solution.py:22
  432.0 4.8 fusion.45
  436.9 0.1 dynamic_update_slice.14
  436.9 4.8 fusion.45
  441.8 0.1 dynamic_update_slice.14
  441.9 4.8 fusion.45
  446.8 0.1 dynamic_update_slice.14
  446.9 4.8 fusion.45
  451.8 0.1 dynamic_update_slice.14
  451.9 41.5 %all-reduce.4 = (f32[2048]{0:T(1024)S(1)}, f32[2048]{0:T(1024)S(1)}) all-reduce(f32[2048]{0:T(1024)S(1)} %bitcast.72, f32[2048]{0:T(1024)S(1)} %bitcast.71), channel_id=3, replica_groups=mesh['row'=16,'col'=8] {'col'}, use_global_device_ids=true, to_apply=%region_16.17.clone | all-reduce | flops 4096 | bytes 32768
  493.4 1.2 fusion.25
  (27 shorter events, 0.5 us)
Async XLA Ops:
  7.2 2.9 copy-start.3
  7.2 242.8 %all-reduce.7.cloned.1.call-start = ((), (), s32[]{:S(2)}) async-start(), calls=%async_computation | async-start | bytes 16777216 | tf_op jit(solution)/shard_map/psum | solution.py:48
  91.8 303.1 %all-gather.4.cloned.1.call-start = ((), (), s32[]{:S(2)}) async-start(), calls=%async_computation.1 | async-start | bytes 1179648 | tf_op jit(solution)/shard_map/all_gather | solution.py:54
  329.4 5.7 %copy-start = (f32[8192,256]{1,0:T(8,128)S(1)}, f32[8192,256]{1,0:T(8,128)}, u32[]{:S(2)}) copy-start(f32[8192,256]{1,0:T(8,128)} %all-reduce.7.cloned.1.call-done) | copy-start | bytes 25165828
  341.8 5.5 %copy-start.1 = (bf16[256,8192]{1,0:T(8,128)(2,1)S(1)}, bf16[256,8192]{1,0:T(8,128)(2,1)}, u32[]{:S(2)}) copy-start(bf16[256,8192]{1,0:T(8,128)(2,1)} %param.6) | copy-start | bytes 12582916
  345.9 1.3 copy-start.2
  347.3 21.8 %copy-start.4 = (u32[128]{0:T(128)S(1)}, u32[128]{0:T(128)}, u32[]{:S(2)}) copy-start(u32[128]{0:T(128)} %constant.145) | copy-start | bytes 1540
  349.4 80.3 %all-gather.6.cloned.1.call-start = ((), (), s32[]{:S(2)}) async-start(), calls=%async_computation.2 | async-start | bytes 2228224 | tf_op jit(solution)/shard_map/all_gather | solution.py:56
Sparse Core Ops, SparseCore 0:
  91.9 157.9 all-reduce.6
  349.5 45.3 all-gather.3
  397.2 32.4 all-gather.5
where the time goes:
time: 507 us; the launch traced here: 501 us
  waiting for transfers between devices  206 us (41%)
  blocking collectives  128 us (25%)
  matrix products  70.5 us (14%)
  other arithmetic  66.2 us (13%)
  between operations  17.5 us (3%)
  local copies, waits for them, and re-layouts  13 us (3%)
    psum x1, waiting for transfers between devices, local(): gram = lax.psum(gram_part, ('row', 'col'))  158 us
    psum x1, blocking collectives, local(): lax.psum((jnp.sum(samples, 0, dtype=jnp.float32), jnp.sum(is_ref)), ('row...  68.6 us
    unnamed x1, blocking collectives  41.5 us
    another operation x6, other arithmetic, local(): factor = jnp.linalg.cholesky(square)  34 us
    all_gather x1, waiting for transfers between devices, local(): lax.all_gather(projected, 'row', axis=0, tiled=True)  33.2 us
    another operation x3, other arithmetic, local(): jax.scipy.linalg.solve_triangular(factor, gram.T, lower=True)  19.9 us
    dot_general x1, matrix products, local(): square = jnp.dot(gram.T, gram, precision=lax.Precision.HIGHEST)  19.5 us
    dot_general x4, matrix products, block_sums(): lax.dot_general(block_rows, panel_cols, (((1,), (1,)), ((), ())), preferr...  19.4 us
  transfers between devices with their start and end apart: 3, of which 3 were waited for; matrix products, arithmetic and copies ran while one was open for 2% of the time, Pallas kernels for 0%

commit v1 on v0

--- a/solution.py
+++ b/solution.py
@@ -45,7 +45,7 @@
         )
         / n_total
     )
-    gram = lax.psum(gram_part, ("row", "col"))
+    gram = lax.psum(lax.psum(gram_part, "col"), "row")
     square = jnp.dot(gram.T, gram, precision=lax.Precision.HIGHEST)
     factor = jnp.linalg.cholesky(square)
     basis = jax.scipy.linalg.solve_triangular(factor, gram.T, lower=True).T.astype(jnp.bfloat16)

time: 507 us -> 729 us (1.44)
  waiting for transfers between devices: 206 us -> 425 us
    psum x1 -> x2, waiting for transfers between devices: 158 us -> 375 us  [local(): gram = lax.psum(lax.psum(gram_part, 'col'), 'row')]
  transfers between devices with their start and end apart: 3 -> 4, of which waited for: 3 -> 4; matrix products, arithmetic and copies ran while one was open for 2% -> 2% of each run, Pallas kernels for 0% -> 0%
where the time goes in v1:
time: 729 us; the launch traced here: 723 us
  waiting for transfers between devices  425 us (58%)
  blocking collectives  130 us (18%)
  matrix products  70.8 us (10%)
  other arithmetic  66.3 us (9%)
  between operations  17.5 us (2%)
  local copies, waits for them, and re-layouts  13 us (2%)
    psum x2, waiting for transfers between devices, local(): gram = lax.psum(lax.psum(gram_part, 'col'), 'row')  375 us
    psum x1, blocking collectives, local(): lax.psum((jnp.sum(samples, 0, dtype=jnp.float32), jnp.sum(is_ref)), ('row...  68.6 us
    unnamed x1, blocking collectives  41.6 us
    another operation x6, other arithmetic, local(): factor = jnp.linalg.cholesky(square)  34 us
    all_gather x1, waiting for transfers between devices, local(): lax.all_gather(projected, 'row', axis=0, tiled=True)  33 us
    another operation x3, other arithmetic, local(): jax.scipy.linalg.solve_triangular(factor, gram.T, lower=True)  19.9 us
    all_gather x1, blocking collectives, local(): lax.all_gather(is_ref.astype(jnp.bfloat16), 'row', axis=0, tiled=True)  19.9 us
    dot_general x1, matrix products, local(): square = jnp.dot(gram.T, gram, precision=lax.Precision.HIGHEST)  19.8 us
  transfers between devices with their start and end apart: 4, of which 4 were waited for; matrix products, arithmetic and copies ran while one was open for 2% of the time, Pallas kernels for 0%

profile of v1, /device:TPU:0, one launch (start us, length us, event | category | flops | bytes accessed | tf_op | source)
XLA Modules:
  0.0 723.4 jit_solution(13633976410314339938)
XLA Ops:
  7.2 0.0 copy-start.3
  7.2 0.0 all-reduce.8.cloned.1.call-start
  7.2 2.9 convert_reduce_fusion
  10.1 0.0 copy-done.3
  10.1 0.6 fusion.26
  10.7 68.6 %all-reduce.3 = (f32[8192]{0:T(1024)S(1)}, f32[]{:T(128)}) all-reduce(f32[8192]{0:T(1024)S(1)} %convert_reduce_fusion, f32[]{:T(128)} %fusion.26), channel_id=1, replica_groups=mesh['row'=16,'col'=8] {'row','col'}, use_global_device_ids=true, to_apply=%region_1.0 | all-reduce | flops 8193 | bytes 65544 | tf_op jit(solution)/shard_map/psum | solution.py:35
  79.3 12.5 %convolution_multiply_fusion = f32[8192,256]{1,0:T(8,128)} fusion(bf16[256,8192]{1,0:T(8,128)(2,1)} %param.6, f32[8192]{0:T(1024)S(1)} %broadcast_multiply_fusion, bf16[8192,256]{1,0:T(8,128)(2,1)} %param.8), kind=kOutput, calls=%fused_computation.8 | convolution fusion | flops 2162229248 | bytes 16809984 | tf_op jit(solution)/shard_map/dot_general | solution.py:43
  91.8 0.0 all-reduce.8.cloned.1.call-update
  91.8 0.0 all-reduce.10.cloned.1.call-start
  91.9 182.2 %all-reduce.8.cloned.1.call-done = f32[8192,256]{1,0:T(8,128)} async-done(((f32[8192,256]{1,0:T(8,128)}), f32[8192,256]{1,0:T(8,128)}) %all-reduce.8.cloned.1.call-update) | async-done | bytes 8388624 | tf_op jit(solution)/shard_map/psum | solution.py:48
  274.1 0.0 all-reduce.10.cloned.1.call-update
  274.1 0.3 all-gather.4.cloned.1.call-start
  274.5 193.1 %all-reduce.10.cloned.1.call-done = f32[8192,256]{1,0:T(8,128)} async-done(((f32[8192,256]{1,0:T(8,128)}), f32[8192,256]{1,0:T(8,128)}) %all-reduce.10.cloned.1.call-update) | async-done | bytes 8388624 | tf_op jit(solution)/shard_map/psum | solution.py:48
  467.6 19.8 %fusion.32 = f32[256,256]{1,0:T(8,128)S(1)} fusion(f32[8192,256]{1,0:T(8,128)} %all-reduce.10.cloned.1.call-done), kind=kOutput, calls=%fused_computation.55 | convolution fusion | flops 6442450944 | bytes 8650752 | tf_op jit(solution)/shard_map/dot_general | solution.py:49
  487.4 0.1 copy.9
  487.6 11.7 %cholesky.50 = f32[128,128]{1,0:T(8,128)S(1)} custom-call(f32[128,128]{1,0:T(8,128)S(1)} %cholesky.118), custom_call_target="Cholesky" | custom-call | tf_op jit(solution)/shard_map/jit(cholesky)/cholesky | solution.py:50
  499.3 9.8 %custom-call.15 = f32[1,128,128]{1,2,0:T(8,128)S(1)} custom-call(f32[1,128,128]{2,1,0:T(8,128)S(1)} %get-tuple-element.162), custom_call_target="InvertDiagBlocksLowerTriangular" | custom-call | tf_op jit(solution)/shard_map/jit(cholesky)/cholesky | solution.py:50
  509.2 0.2 constant_dynamic-update-slice_fusion.1
  509.4 0.3 convolution_subtract_fusion.1
  509.7 11.7 %cholesky.105 = f32[128,128]{1,0:T(8,128)S(1)} custom-call(f32[128,128]{1,0:T(8,128)S(1)} %convolution_subtract_fusion.1), custom_call_target="Cholesky" | custom-call | tf_op jit(solution)/shard_map/jit(cholesky)/cholesky | solution.py:50
  521.4 0.6 compare_reduce_fusion
  523.4 0.1 triangular_solve.59
  523.5 4.0 while.16
  523.5 0.6 fusion.46
  524.1 1.4 bitcast_dynamic-update-slice_fusion.2
  525.5 0.6 fusion.46
  526.1 1.4 bitcast_dynamic-update-slice_fusion.2
  527.5 19.8 %custom-call.16 = f32[2,128,128]{1,2,0:T(8,128)S(1)} custom-call(f32[2,128,128]{2,1,0:T(8,128)S(1)} %get-tuple-element.118), custom_call_target="InvertDiagBlocksLowerTriangular" | custom-call | tf_op jit(solution)/shard_map/jit(_solve_triangular)/triangular_solve | solution.py:51
  547.3 0.0 copy-start
  547.3 5.7 fusion.31
  553.0 0.0 copy-done
  553.0 6.7 convolution_subtract_fusion
  559.7 0.0 copy-start.1
  559.7 4.1 convolution_convert_fusion
  563.9 0.0 copy-start.2
  563.9 1.3 copy-done.2
  565.2 0.0 copy-done.1
  565.2 0.0 copy-start.4
  565.2 2.1 fusion.15
  567.3 0.0 all-gather.4.cloned.1.call-update
  567.3 0.0 all-gather.6.cloned.1.call-start
  567.4 0.5 all-gather.6.cloned.1.call-update
  568.0 19.9 %all-gather = bf16[16,1,256]{2,1,0:T(2,128)(2,1)S(1)} all-gather(bf16[1,1,256]{2,1,0:T(2,128)(2,1)S(1)} %reshape.65), channel_id=1, replica_groups=mesh['row'=16,'col'=8] {'row'}, dimensions={0}, use_global_device_ids=true | all-gather | bytes 8704 | tf_op jit(solution)/shard_map/all_gather | solution.py:57
  589.1 0.0 copy-done.4
  589.1 0.7 dynamic-slice.3
  590.5 3.9 fusion.11
  594.4 6.4 copy.10
  600.7 16.3 %all-gather.4.cloned.1.call-done = bf16[2048,256]{1,0:T(8,128)(2,1)} async-done(((bf16[256,256]{1,0:T(8,128)(2,1)}), bf16[2048,256]{1,0:T(8,128)(2,1)}) %all-gather.4.cloned.1.call-update) | async-done | bytes 1048592 | tf_op jit(solution)/shard_map/all_gather | solution.py:54
  617.0 1.6 multiply_reduce_fusion.2
  618.6 33.0 %all-gather.6.cloned.1.call-done = bf16[4096,256]{1,0:T(8,128)(2,1)} async-done(((bf16[256,256]{1,0:T(8,128)(2,1)}), bf16[4096,256]{1,0:T(8,128)(2,1)}) %all-gather.6.cloned.1.call-update) | async-done | bytes 2097168 | tf_op jit(solution)/shard_map/all_gather | solution.py:56
  651.7 2.2 multiply_reduce_fusion.1
  653.9 19.9 %while.15 = (s32[]{:T(128)}, f32[4,512]{1,0:T(4,128)S(1)}, f32[4,512]{1,0:T(4,128)S(1)}, f32[4,512]{1,0:T(4,128)S(1)}, f32[4096]{0:T(1024)S(1)}, /*index=5*/bf16...) while((s32[]{:T(128)}, f32[4,512]{1,0:T(4,128)S(1)}, ...), condition=%wide.region_13.14_spmd, body=%wide.region_10.13_spmd.sunk | while | flops 1090518016 | bytes 2411641 | solution.py:22
  653.9 4.8 fusion.45
  658.8 0.1 dynamic_update_slice.14
  658.9 4.8 fusion.45
  663.8 0.1 dynamic_update_slice.14
  663.8 4.8 fusion.45
  668.7 0.1 dynamic_update_slice.14
  668.8 4.8 fusion.45
  673.7 0.1 dynamic_update_slice.14
  673.8 41.6 %all-reduce.4 = (f32[2048]{0:T(1024)S(1)}, f32[2048]{0:T(1024)S(1)}) all-reduce(f32[2048]{0:T(1024)S(1)} %bitcast.72, f32[2048]{0:T(1024)S(1)} %bitcast.71), channel_id=3, replica_groups=mesh['row'=16,'col'=8] {'col'}, use_global_device_ids=true, to_apply=%region_17.18.clone | all-reduce | flops 4096 | bytes 32768
  715.4 1.2 fusion.25
  (27 shorter events, 0.5 us)
Async XLA Ops:
  7.2 2.9 copy-start.3
  7.2 266.9 %all-reduce.8.cloned.1.call-start = ((), (), s32[]{:S(2)}) async-start(), calls=%async_computation | async-start | bytes 16777216 | tf_op jit(solution)/shard_map/psum | solution.py:48
  91.8 375.7 %all-reduce.10.cloned.1.call-start = ((), (), s32[]{:S(2)}) async-start(), calls=%async_computation.1 | async-start | bytes 16777216 | tf_op jit(solution)/shard_map/psum | solution.py:48
  274.1 342.9 %all-gather.4.cloned.1.call-start = ((), (), s32[]{:S(2)}) async-start(), calls=%async_computation.2 | async-start | bytes 1179648 | tf_op jit(solution)/shard_map/all_gather | solution.py:54
  547.3 5.7 copy-start
  559.7 5.5 copy-start.1
  563.9 1.3 copy-start.2
  565.2 23.9 %copy-start.4 = (u32[128]{0:T(128)S(1)}, u32[128]{0:T(128)}, u32[]{:S(2)}) copy-start(u32[128]{0:T(128)} %constant.145) | copy-start | bytes 1540
  567.3 84.3 %all-gather.6.cloned.1.call-start = ((), (), s32[]{:S(2)}) async-start(), calls=%async_computation.3 | async-start | bytes 2228224 | tf_op jit(solution)/shard_map/all_gather | solution.py:56
Sparse Core Ops, SparseCore 0:
  91.9 182.1 all-reduce.7
  276.6 190.8 all-reduce.9
  567.4 49.5 all-gather.3
  619.1 32.4 all-gather.5
